TPU v7x, 32 devices: a whole 2x2x4 slice. The times are simulated.
32 devices in a mesh: tile: 16 (over z, y, x), mode: 2 (over core).
Axes of the slice: x: 2, y: 2, z: 4, core: 2. Of those that a mesh axis runs over, the one named last changes fastest.
Arguments:
- object_tiles: float32 [2, 2048, 2048], P(None, 'tile'), may hold values from -6 to 6
- probe_modes: float32 [4, 2, 256, 256], P('mode'), may hold values from -5 to 5
- amplitudes: float32 [16, 256, 256], P('tile'), may hold values from 0.25 to 4
- scan_offsets: int32 [8192, 2], replicated, may hold values from 0 to 1792, as said below
- slot_scan: int32 [16], P('tile'), may hold values from 0 to 8191, as said below
- slot_count: int32 [16], P('tile'), may hold values from 0 to 1, as said below
Outputs:
- updated_object: float32 [2, 2048, 2048], P(None, 'tile')
- object_gradient: float32 [2, 2048, 2048], P(None, 'tile')
Inputs may be any that keep to these rules, and one draw needn't show every extreme that they name: `scan_offsets`: every patch of 256 x 256 pixels at an offset lies inside the object. `slot_scan`: on every index d of tile but the last, the row offset of each slot's scan position lies in [d * 128, (d + 1) * 128). The positions of one device's slots are distinct. `slot_count`: the live slots of a device are its first ones. The last index of tile holds none, every other holds at least one; some index holds 1.
All inputs are finite; a program needn't handle non-finite values.
Results may differ from a plain program's by a relative error of at most 0.0001.
Values sent between devices are 32-bit elements; how exact they have to be, the bound alone decides.
No kernel may reach another device: no remote copies, remote signals or barrier semaphores. Data moves between devices by JAX's collectives and lax.ppermute only.
A program may use at most 64 MiB of HBM per device.

v0:
```python
import math
import jax
import jax.numpy as jnp
from jax import lax
from jax.sharding import PartitionSpec as P

FLOOR = 0.25
ALPHA = 0.5


def from_behind(value, axis, steps):
    count = lax.axis_size(axis)
    initial, last = (max(0, -steps), min(count, count - steps))
    return lax.ppermute(value, axis, [(source, source + steps) for source in range(initial, last)])


def tables(frame):
    index = jnp.arange(frame, dtype=jnp.int32)
    phase = (index[:, None] * index[None, :] % frame).astype(jnp.float32) * (2.0 * math.pi / frame)
    scale = 1.0 / math.sqrt(frame)
    return (jnp.cos(phase) * scale, -jnp.sin(phase) * scale)


def product(first, second):
    return jnp.matmul(first, second, precision=lax.Precision.HIGHEST)


def transform(real_part, imag_part, cos_table, sin_table):
    inner_re = product(cos_table, real_part) - product(sin_table, imag_part)
    inner_im = product(cos_table, imag_part) + product(sin_table, real_part)
    outer_re = product(inner_re, cos_table) - product(inner_im, sin_table)
    outer_im = product(inner_im, cos_table) + product(inner_re, sin_table)
    return (outer_re, outer_im)


def shards(object_tiles, probe_modes, amplitudes, scan_offsets, slot_scan, slot_count):
    height = object_tiles.shape[1]
    breadth = object_tiles.shape[2]
    frame = probe_modes.shape[2]
    slot_total = slot_scan.shape[0]
    device = lax.axis_index("tile")
    anchor = jnp.zeros((), jnp.int32)
    cos_table, sin_table = tables(frame)
    probe_re = probe_modes[:, 0]
    probe_im = probe_modes[:, 1]
    illumination = lax.psum(jnp.sum(probe_re * probe_re + probe_im * probe_im, axis=0), "mode")
    offsets = jnp.take(scan_offsets, slot_scan, axis=0)
    row_start = offsets[:, 0] - device * height
    col_start = offsets[:, 1]
    active = (jnp.arange(slot_total, dtype=jnp.int32) < slot_count[0]).astype(jnp.float32)

    def cut_columns(col_at):
        return lax.dynamic_slice(object_tiles, (anchor, anchor, col_at), (2, height, frame))

    their_starts = []
    pieces = [jax.vmap(cut_columns)(col_start)]
    for distance in (1, 2):
        remote = from_behind(col_start, "tile", distance)
        their_starts.append(remote)
        windows = jax.vmap(cut_columns)(remote)
        pieces.append(from_behind(windows, "tile", -distance))
    canvas = jnp.concatenate(pieces, axis=2)

    def cut_rows(column_block, row_at):
        return lax.dynamic_slice(column_block, (anchor, row_at, anchor), (2, frame, frame))

    patches = jax.vmap(cut_rows)(canvas, row_start)
    patch_re = patches[:, 0][:, None]
    patch_im = patches[:, 1][:, None]
    wave_re = probe_re[None] * patch_re - probe_im[None] * patch_im
    wave_im = probe_re[None] * patch_im + probe_im[None] * patch_re
    far_re, far_im = transform(wave_re, wave_im, cos_table, sin_table)
    intensity = lax.psum(jnp.sum(far_re * far_re + far_im * far_im, axis=1), "mode")
    factor = (amplitudes / jnp.sqrt(jnp.maximum(intensity, FLOOR)))[:, None]
    back_re, back_im = transform(far_re * factor, far_im * factor, cos_table, -sin_table)
    delta_re = back_re - wave_re
    delta_im = back_im - wave_im
    weights = active[:, None, None]
    grad_re = jnp.sum(probe_re[None] * delta_re + probe_im[None] * delta_im, axis=1) * weights
    grad_im = jnp.sum(probe_re[None] * delta_im - probe_im[None] * delta_re, axis=1) * weights
    coverage = illumination[None] * weights
    contribution = jnp.stack([grad_re, grad_im, coverage], axis=1)
    channels = contribution.shape[1]

    def place(piece, row_at):
        empty = jnp.zeros((channels, 3 * height, frame), jnp.float32)
        return lax.dynamic_update_slice(empty, piece, (anchor, row_at, anchor))

    padded = jax.vmap(place)(contribution, row_start)
    blocks = [(padded[:, :, :height], col_start)]
    for distance in (1, 2):
        arrived = from_behind(
            padded[:, :, distance * height : (distance + 1) * height], "tile", distance
        )
        blocks.append((arrived, their_starts[distance - 1]))
    totals = jnp.zeros((channels, height, breadth), jnp.float32)
    for block, starts in blocks:

        def add_block(index, accum, block=block, starts=starts):
            current = lax.dynamic_slice(
                accum, (anchor, anchor, starts[index]), (channels, height, frame)
            )
            return lax.dynamic_update_slice(
                accum, current + block[index], (anchor, anchor, starts[index])
            )

        totals = lax.fori_loop(0, slot_total, add_block, totals)
    cover = totals[2]
    gradient = totals[:2]
    gradient = lax.psum(gradient, "mode")
    updated = object_tiles + gradient / (cover + ALPHA)
    return (updated, gradient)


def solution(mesh):
    return jax.shard_map(
        shards,
        mesh=mesh,
        in_specs=(
            P(None, "tile", None),
            P("mode", None, None, None),
            P("tile", None, None),
            P(),
            P("tile"),
            P("tile"),
        ),
        out_specs=(P(None, "tile", None), P(None, "tile", None)),
        check_vma=False,
    )
```

profile of v0, /device:TPU:0, one launch (start us, length us, event | category | flops | bytes accessed | tf_op | source)
XLA Modules:
  0.0 183.3 jit_solution(3276640202237334104)
XLA Ops:
  9.2 5.5 %collective-permute-start.2 = (s32[1]{0:T(128)}, s32[1]{0:T(128)}, u32[]{:S(2)}, u32[]{:S(2)}) collective-permute-start(s32[1]{0:T(128)} %bitcast.10), channel_id=1, source_target_pairs={{0,4},{2,6},{4,8},{6,10},{8,12},{10,14},{12,16},{14,18},{16,20},{1... | collective-permute-start | bytes 20 | tf_op jit(solution)/shard_map/ppermute | solution.py:14
  14.7 3.9 %collective-permute-start = (s32[1]{0:T(128)}, s32[1]{0:T(128)}, u32[]{:S(2)}, u32[]{:S(2)}) collective-permute-start(s32[1]{0:T(128)} %bitcast.10), channel_id=1, source_target_pairs={{0,2},{2,4},{4,6},{6,8},{8,10},{10,12},{12,14},{14,16},{16,18},{18... | collective-permute-start | bytes 20 | tf_op jit(solution)/shard_map/ppermute | solution.py:14
  24.1 1.7 dynamic-slice_bitcast_fusion
  29.1 6.1 %collective-permute-done.3 = f32[1,2,128,256]{3,2,1,0:T(8,128)S(1)} collective-permute-done((f32[1,2,128,256]{3,2,1,0:T(8,128)S(1)}, f32[1,2,128,256]{3,2,1,0:T(8,128)S(1)}, u32[]{:S(2)}, u32[]{:S(2)}) %collective-permute-start.3) | collective-permute-done | bytes 262176 | tf_op jit(solution)/shard_map/ppermute | solution.py:14
  36.9 1.6 fusion.46
  38.6 1.6 fusion.42
  40.2 1.6 fusion.5
  41.9 1.6 fusion.44
  43.4 1.6 fusion.4
  45.1 1.6 fusion.40
  46.7 1.6 convolution_subtract_fusion.2
  48.2 2.5 %add_reduce_fusion = (f32[256,256]{1,0:T(8,128)}, f32[2,256,256]{2,1,0:T(8,128)S(1)}) fusion(f32[2,256,256]{2,1,0:T(8,128)S(1)} %convolution_subtract_fusion.2, f32[2,256,256]{2,1,0:T(8,128)S(1)} %fusion.40, f32[2,256,256]{2,1,0:T(8,128)S(1)} %fusion.5), kind=kOutput, calls=%fused_computation.41 | convolution fusion | flops 404291584 | bytes 2359296 | tf_op jit(solution)/shard_map/dot_general | solution.py:25
  51.5 21.8 %all-reduce.7.cloned.1.call-done = f32[1,256,256]{2,1,0:T(8,128)} async-done(((f32[1,256,256]{2,1,0:T(8,128)}), f32[1,256,256]{2,1,0:T(8,128)}) %all-reduce.7.cloned.1.call-update) | async-done | bytes 262160 | tf_op jit(solution)/shard_map/psum | solution.py:73
  74.3 1.6 fusion.21
  76.0 1.7 fusion.17
  77.6 1.7 fusion.2
  79.3 1.7 fusion.3
  81.0 1.6 fusion.37
  82.5 1.6 fusion.34
  84.1 1.6 fusion.1
  85.7 2.6 %fusion.12 = (f32[256,256]{1,0:T(8,128)S(1)}, f32[256,256]{1,0:T(8,128)S(1)}, f32[256,256]{1,0:T(8,128)}) fusion(f32[2,256,256]{2,1,0:T(8,128)S(1)} %fusion.1, f32[2,2,256,256]{3,2,1,0:T(8,128)S(1)} %copy-done.1, f32[2,256,256]{2,1,0:T(8,128)S(1)} %get-tuple-element.121, f32[2,256,256]{2,1,0:T(8,128)S(1)} %fusion.34, f32[2,256,256]{2,1,0:T(8,128)S(1)} %fusion.3), kind=kOutput, calls=%fused_computation.31 | convolution fusion | flops 405405696 | bytes 3932160 | tf_op jit(solution)/shard_map/dot_general | solution.py:25
  88.4 2.7 %and_reduce_fusion = pred[]{:T(512)} fusion(s32[4]{0:T(128)S(1)} %copy-done.3, s32[1]{0:T(128)} %bitcast.7, s32[1]{0:T(128)} %bitcast.6, s32[1]{0:T(128)} %bitcast.5, s32[1]{0:T(128)} %constant.96.clone.1), kind=kLoop, calls=%fused_computation.118 | loop fusion | flops 27 | bytes 33 | tf_op jit(solution)/shard_map/reduce.1
  91.8 16.2 %all-reduce.9.cloned.1.call-done = f32[256,256]{1,0:T(8,128)} async-done(((f32[256,256]{1,0:T(8,128)}), f32[256,256]{1,0:T(8,128)}) %all-reduce.9.cloned.1.call-update) | async-done | bytes 262160 | tf_op jit(solution)/shard_map/psum | solution.py:46
  109.7 4.8 %scatter.4 = f32[1,3,384,256]{3,2,1,0:T(8,128)S(1)} dynamic-update-slice(f32[1,3,384,256]{3,2,1,0:T(8,128)S(1)} %broadcast_in_dim.32, f32[1,3,256,256]{3,2,1,0:T(8,128)S(1)} %maximum_select_fusion, s32[]{:T(128)} %constant.95.clone.1, s32[]{:T(128)} %constant.95.clone.1, s32[]{:T(128)} %bitcast.49, s32[]{:T(128)} %constant.95.clone.1) | dynamic-update-slice | bytes 1572868 | tf_op jit(solution)/shard_map/vmap(vmap())/scatter | solution.py:87
  115.5 3.8 %collective-permute-start.4 = (f32[1,3,128,256]{3,2,1,0:T(8,128)}, f32[1,3,128,256]{3,2,1,0:T(8,128)}, u32[]{:S(2)}, u32[]{:S(2)}) collective-permute-start(f32[1,3,128,256]{3,2,1,0:T(8,128)} %get-tuple-element.123), channel_id=1, source_target_pairs={{0,2},{2,4},{4,6},{6,8},{8,10},{10,12},{12,14},{14,16},{16,18},{18... | collective-permute-start | bytes 1179656 | tf_op jit(solution)/shard_map/ppermute | solution.py:14
  119.3 3.8 %collective-permute-start.5 = (f32[1,3,128,256]{3,2,1,0:T(8,128)}, f32[1,3,128,256]{3,2,1,0:T(8,128)}, u32[]{:S(2)}, u32[]{:S(2)}) collective-permute-start(f32[1,3,128,256]{3,2,1,0:T(8,128)} %get-tuple-element.122), channel_id=1, source_target_pairs={{0,4},{2,6},{4,8},{6,10},{8,12},{10,14},{12,16},{14,18},{16,20},{1... | collective-permute-start | bytes 1179656 | tf_op jit(solution)/shard_map/ppermute | solution.py:14
  128.9 4.8 %dynamic_update_slice.12 = f32[3,128,2048]{2,1,0:T(8,128)S(1)} dynamic-update-slice(f32[3,128,2048]{2,1,0:T(8,128)S(1)} %broadcast_in_dim.31, f32[3,128,256]{2,1,0:T(8,128)S(1)} %get-tuple-element.124, s32[]{:T(128)} %constant.95.clone.1, s32[]{:T(128)} %constant.95.clone.1, s32[]{:T(128)S(6)} %select_n.101) | dynamic-update-slice | bytes 786436 | tf_op jit(solution)/shard_map/while/body/eval_jaxpr/dynamic_update_slice | solution.py:103
  134.9 4.8 %dynamic_update_slice.13 = f32[3,128,2048]{2,1,0:T(8,128)S(1)} dynamic-update-slice(f32[3,128,2048]{2,1,0:T(8,128)S(1)} %dynamic_update_slice.12, f32[3,128,256]{2,1,0:T(8,128)S(1)} %bitcast_add_fusion.1, s32[]{:T(128)} %constant.95.clone.1, s32[]{:T(128)} %constant.95.clone.1, s32[]{:T(128)S(6)} %select_n.102) | dynamic-update-slice | bytes 786436 | tf_op jit(solution)/shard_map/while/body/eval_jaxpr/dynamic_update_slice | solution.py:103
  141.0 4.8 %dynamic_update_slice.14 = f32[3,128,2048]{2,1,0:T(8,128)S(1)} dynamic-update-slice(f32[3,128,2048]{2,1,0:T(8,128)S(1)} %dynamic_update_slice.13, f32[3,128,256]{2,1,0:T(8,128)S(1)} %bitcast_add_fusion, s32[]{:T(128)} %constant.95.clone.1, s32[]{:T(128)} %constant.95.clone.1, s32[]{:T(128)S(6)} %select_n.103) | dynamic-update-slice | bytes 786436 | tf_op jit(solution)/shard_map/while/body/eval_jaxpr/dynamic_update_slice | solution.py:103
  145.8 1.5 slice.166
  148.3 22.6 %all-reduce.11.cloned.1.call-done = f32[2,128,2048]{2,1,0:T(8,128)} async-done(((f32[2,128,2048]{2,1,0:T(8,128)}), f32[2,128,2048]{2,1,0:T(8,128)}) %all-reduce.11.cloned.1.call-update) | async-done | bytes 2097168 | tf_op jit(solution)/shard_map/psum | solution.py:110
  171.0 4.5 %divide_add_fusion = f32[2,128,2048]{2,1,0:T(8,128)} fusion(f32[2,128,2048]{2,1,0:T(8,128)} %param.8, f32[2,128,2048]{2,1,0:T(8,128)} %all-reduce.11.cloned.1.call-done, f32[128,2048]{1,0:T(8,128)} %fusion.6), kind=kLoop, calls=%fused_computation | loop fusion | flops 1048576 | bytes 7340032 | tf_op jit(solution)/shard_map/add | solution.py:111
  (41 shorter events, 15.3 us)
Async XLA Ops:
  7.2 29.6 %copy-start.1 = (f32[2,2,256,256]{3,2,1,0:T(8,128)S(1)}, f32[2,2,256,256]{3,2,1,0:T(8,128)}, u32[]{:S(2)}) copy-start(f32[2,2,256,256]{3,2,1,0:T(8,128)} %param.9) | copy-start | bytes 3145732
  7.2 66.1 %all-reduce.7.cloned.1.call-start = ((), (), s32[]{:S(2)}) async-start(), calls=%async_computation | async-start | bytes 524288 | tf_op jit(solution)/shard_map/psum | solution.py:73
  9.2 11.1 %collective-permute-start.2 = (s32[1]{0:T(128)}, s32[1]{0:T(128)}, u32[]{:S(2)}, u32[]{:S(2)}) collective-permute-start(s32[1]{0:T(128)} %bitcast.10), channel_id=1, source_target_pairs={{0,4},{2,6},{4,8},{6,10},{8,12},{10,14},{12,16},{14,18},{16,20},{1... | collective-permute-start | bytes 20 | tf_op jit(solution)/shard_map/ppermute | solution.py:14
  14.7 7.0 %collective-permute-start = (s32[1]{0:T(128)}, s32[1]{0:T(128)}, u32[]{:S(2)}, u32[]{:S(2)}) collective-permute-start(s32[1]{0:T(128)} %bitcast.10), channel_id=1, source_target_pairs={{0,2},{2,4},{4,6},{6,8},{8,10},{10,12},{12,14},{14,16},{16,18},{18... | collective-permute-start | bytes 20 | tf_op jit(solution)/shard_map/ppermute | solution.py:14
  25.8 9.4 %collective-permute-start.3 = (f32[1,2,128,256]{3,2,1,0:T(8,128)S(1)}, f32[1,2,128,256]{3,2,1,0:T(8,128)S(1)}, u32[]{:S(2)}, u32[]{:S(2)}) collective-permute-start(f32[1,2,128,256]{3,2,1,0:T(8,128)S(1)} %get-tuple-element.117), channel_id=1, source_target_pairs={{4,0},{6,2},{8,4},{10,6},{12,8},{14,10},{16,12},{18,14},{20,16},{2... | collective-permute-start | bytes 786440 | tf_op jit(solution)/shard_map/ppermute | solution.py:14
  27.1 9.4 %collective-permute-start.1 = (f32[1,2,128,256]{3,2,1,0:T(8,128)S(1)}, f32[1,2,128,256]{3,2,1,0:T(8,128)S(1)}, u32[]{:S(2)}, u32[]{:S(2)}) collective-permute-start(f32[1,2,128,256]{3,2,1,0:T(8,128)S(1)} %get-tuple-element.118), channel_id=1, source_target_pairs={{2,0},{4,2},{6,4},{8,6},{10,8},{12,10},{14,12},{16,14},{18,16},{20... | collective-permute-start | bytes 786440 | tf_op jit(solution)/shard_map/ppermute | solution.py:14
  46.6 4.1 %copy-start.4 = (s32[1,3]{1,0:T(1,128)S(1)}, s32[1,3]{1,0:T(1,128)}, u32[]{:S(2)}) copy-start(s32[1,3]{1,0:T(1,128)} %constant.105.clone.1) | copy-start | bytes 40
  46.7 26.7 %copy-start.2 = (f32[1,256,256]{2,1,0:T(8,128)S(1)}, f32[1,256,256]{2,1,0:T(8,128)}, u32[]{:S(2)}) copy-start(f32[1,256,256]{2,1,0:T(8,128)} %param.10) | copy-start | bytes 786436
  50.7 57.2 %all-reduce.9.cloned.1.call-start = ((), (), s32[]{:S(2)}) async-start(), calls=%async_computation.1 | async-start | bytes 524288 | tf_op jit(solution)/shard_map/psum | solution.py:46
  85.7 2.7 %copy-start.3 = (s32[4]{0:T(128)S(1)}, s32[4]{0:T(128)}, u32[]{:S(2)}) copy-start(s32[4]{0:T(128)} %constant.106.clone.1) | copy-start | bytes 52
  88.3 82.6 %all-reduce.11.cloned.1.call-start = ((), (), s32[]{:S(2)}) async-start(), calls=%async_computation.2 | async-start | bytes 4194304 | tf_op jit(solution)/shard_map/psum | solution.py:110
  115.5 18.3 %collective-permute-start.4 = (f32[1,3,128,256]{3,2,1,0:T(8,128)}, f32[1,3,128,256]{3,2,1,0:T(8,128)}, u32[]{:S(2)}, u32[]{:S(2)}) collective-permute-start(f32[1,3,128,256]{3,2,1,0:T(8,128)} %get-tuple-element.123), channel_id=1, source_target_pairs={{0,2},{2,4},{4,6},{6,8},{8,10},{10,12},{12,14},{14,16},{16,18},{18... | collective-permute-start | bytes 1179656 | tf_op jit(solution)/shard_map/ppermute | solution.py:14
  119.3 20.5 %collective-permute-start.5 = (f32[1,3,128,256]{3,2,1,0:T(8,128)}, f32[1,3,128,256]{3,2,1,0:T(8,128)}, u32[]{:S(2)}, u32[]{:S(2)}) collective-permute-start(f32[1,3,128,256]{3,2,1,0:T(8,128)} %get-tuple-element.122), channel_id=1, source_target_pairs={{0,4},{2,6},{4,8},{6,10},{8,12},{10,14},{12,16},{14,18},{16,20},{1... | collective-permute-start | bytes 1179656 | tf_op jit(solution)/shard_map/ppermute | solution.py:14
  170.9 4.5 %copy-start = (f32[2,128,2048]{2,1,0:T(8,128)S(1)}, f32[2,128,2048]{2,1,0:T(8,128)}, u32[]{:S(2)}) copy-start(f32[2,128,2048]{2,1,0:T(8,128)} %all-reduce.11.cloned.1.call-done) | copy-start | bytes 6291460
Sparse Core Ops, SparseCore 0:
  50.9 22.4 all-reduce.6
  88.5 19.4 all-reduce.8
  147.4 23.5 all-reduce.10
where the time goes:
time: 184 us; the launch traced here: 183 us
  waiting for transfers between devices  68.1 us (37%)
  matrix products  27.6 us (15%)
  between operations  27.1 us (15%)
  local copies, waits for them, and re-layouts  26.4 us (14%)
  starting transfers between devices  19.7 us (11%)
  other arithmetic  14.4 us (8%)
    dot_general x16, matrix products, product(): return jnp.matmul(first, second, precision=lax.Precision.HIGHEST)  27.6 us
    psum x1, waiting for transfers between devices, shards(): gradient = lax.psum(gradient, 'mode')  22.6 us
    psum x1, waiting for transfers between devices, shards(): lax.psum(jnp.sum(far_re * far_re + far_im * far_im, axis=1), 'mode')  21.8 us
    ppermute x6, starting transfers between devices, from_behind(): lax.ppermute(value, axis, [(source, source + steps) for source in range(i...  19.6 us
    psum x1, waiting for transfers between devices, shards(): lax.psum(jnp.sum(probe_re * probe_re + probe_im * probe_im, axis=0), 'mode')  16.2 us
    dynamic_update_slice x3, local copies, waits for them, and re-layouts, add_block(): lax.dynamic_update_slice(accum, current + block[index], (anchor, anchor,...  14.5 us
    ppermute x6, waiting for transfers between devices, from_behind(): lax.ppermute(value, axis, [(source, source + steps) for source in range(i...  7.43 us
    scatter x1, local copies, waits for them, and re-layouts, place(): return lax.dynamic_update_slice(empty, piece, (anchor, row_at, anchor))  4.77 us
  transfers between devices with their start and end apart: 9, of which 5 were waited for; matrix products, arithmetic and copies ran while one was open for 9% of the time, Pallas kernels for 0%

commit v1 on v0

--- a/solution.py
+++ b/solution.py
@@ -43,7 +43,9 @@
     cos_table, sin_table = tables(frame)
     probe_re = probe_modes[:, 0]
     probe_im = probe_modes[:, 1]
-    illumination = lax.psum(jnp.sum(probe_re * probe_re + probe_im * probe_im, axis=0), "mode")
+    part = jnp.sum(probe_re * probe_re + probe_im * probe_im, axis=0)
+    shards_2 = lax.all_gather(part, "mode")
+    illumination = jnp.sum(shards_2, axis=0)
     offsets = jnp.take(scan_offsets, slot_scan, axis=0)
     row_start = offsets[:, 0] - device * height
     col_start = offsets[:, 1]

time: 184 us -> 166 us (0.902)
  waiting for transfers between devices: 68.1 us -> 48.5 us
  blocking collectives: 0 us -> 2.18 us
    psum x1 -> x0, waiting for transfers between devices: 16.2 us -> none  [shards(): lax.psum(jnp.sum(probe_re * probe_re + probe_im * probe_im, axis=0), 'mode')]
    psum x1, waiting for transfers between devices: 21.8 us -> 18.5 us  [shards(): lax.psum(jnp.sum(far_re * far_re + far_im * far_im, axis=1), 'mode')]
    all_gather x0 -> x1, blocking collectives: none -> 2.18 us  [shards(): shards_2 = lax.all_gather(part, 'mode')]
  transfers between devices with their start and end apart: 9 -> 8, of which waited for: 5 -> 4; matrix products, arithmetic and copies ran while one was open for 9% -> 9% of each run, Pallas kernels for 0% -> 0%
where the time goes in v1:
time: 166 us; the launch traced here: 165 us
  waiting for transfers between devices  48.5 us (29%)
  between operations  27.7 us (17%)
  matrix products  26.9 us (16%)
  local copies, waits for them, and re-layouts  26.5 us (16%)
  starting transfers between devices  19.6 us (12%)
  other arithmetic  13.5 us (8%)
  blocking collectives  2.18 us (1%)
    dot_general x16, matrix products, product(): return jnp.matmul(first, second, precision=lax.Precision.HIGHEST)  26.9 us
    psum x1, waiting for transfers between devices, shards(): gradient = lax.psum(gradient, 'mode')  22.5 us
    ppermute x6, starting transfers between devices, from_behind(): lax.ppermute(value, axis, [(source, source + steps) for source in range(i...  19.5 us
    psum x1, waiting for transfers between devices, shards(): lax.psum(jnp.sum(far_re * far_re + far_im * far_im, axis=1), 'mode')  18.5 us
    dynamic_update_slice x3, local copies, waits for them, and re-layouts, add_block(): lax.dynamic_update_slice(accum, current + block[index], (anchor, anchor,...  14.5 us
    ppermute x6, waiting for transfers between devices, from_behind(): lax.ppermute(value, axis, [(source, source + steps) for source in range(i...  7.43 us
    scatter x1, local copies, waits for them, and re-layouts, place(): return lax.dynamic_update_slice(empty, piece, (anchor, row_at, anchor))  4.84 us
    add x1, other arithmetic, shards(): updated = object_tiles + gradient / (cover + ALPHA)  4.51 us
  transfers between devices with their start and end apart: 8, of which 4 were waited for; matrix products, arithmetic and copies ran while one was open for 9% of the time, Pallas kernels for 0%

profile of v1, /device:TPU:0, one launch (start us, length us, event | category | flops | bytes accessed | tf_op | source)
XLA Modules:
  0.0 165.0 jit_solution(13570193522093173880)
XLA Ops:
  9.3 5.4 %collective-permute-start.2 = (s32[1]{0:T(128)}, s32[1]{0:T(128)}, u32[]{:S(2)}, u32[]{:S(2)}) collective-permute-start(s32[1]{0:T(128)} %bitcast.10), channel_id=1, source_target_pairs={{0,4},{2,6},{4,8},{6,10},{8,12},{10,14},{12,16},{14,18},{16,20},{1... | collective-permute-start | bytes 20 | tf_op jit(solution)/shard_map/ppermute | solution.py:14
  14.7 3.9 %collective-permute-start = (s32[1]{0:T(128)}, s32[1]{0:T(128)}, u32[]{:S(2)}, u32[]{:S(2)}) collective-permute-start(s32[1]{0:T(128)} %bitcast.10), channel_id=1, source_target_pairs={{0,2},{2,4},{4,6},{6,8},{8,10},{10,12},{12,14},{14,16},{16,18},{18... | collective-permute-start | bytes 20 | tf_op jit(solution)/shard_map/ppermute | solution.py:14
  24.3 1.7 %dynamic-slice_bitcast_fusion = (f32[1,2,128,256]{3,2,1,0:T(8,128)S(1)}, f32[1,2,128,256]{3,2,1,0:T(8,128)S(1)}, f32[1,2,128,256]{3,2,1,0:T(8,128)S(1)}) fusion(f32[2,128,2048]{2,1,0:T(8,128)} %param.8, s32[]{:T(128)} %bitcast.15, s32[]{:T(128)} %bitcast.13, s32[]{:T(128)} %bitcast.11), kind=kLoop, calls=%fused_computation.81 | loop fusion | bytes 1572876 | tf_op jit(solution)/shard_map/vmap()/gather | solution.py:55
  29.3 6.1 %collective-permute-done.3 = f32[1,2,128,256]{3,2,1,0:T(8,128)S(1)} collective-permute-done((f32[1,2,128,256]{3,2,1,0:T(8,128)S(1)}, f32[1,2,128,256]{3,2,1,0:T(8,128)S(1)}, u32[]{:S(2)}, u32[]{:S(2)}) %collective-permute-start.3) | collective-permute-done | bytes 262176 | tf_op jit(solution)/shard_map/ppermute | solution.py:14
  37.1 1.6 fusion.46
  38.8 1.6 fusion.42
  40.4 1.6 fusion.5
  42.0 1.6 fusion.44
  43.6 1.6 fusion.4
  45.3 1.6 fusion.40
  46.9 1.6 convolution_subtract_fusion.2
  48.4 2.5 %add_reduce_fusion = (f32[256,256]{1,0:T(8,128)}, f32[2,256,256]{2,1,0:T(8,128)S(1)}) fusion(f32[2,256,256]{2,1,0:T(8,128)S(1)} %convolution_subtract_fusion.2, f32[2,256,256]{2,1,0:T(8,128)S(1)} %fusion.40, f32[2,256,256]{2,1,0:T(8,128)S(1)} %fusion.5), kind=kOutput, calls=%fused_computation.41 | convolution fusion | flops 404291584 | bytes 2359296 | tf_op jit(solution)/shard_map/dot_general | solution.py:25
  52.4 2.7 %and_reduce_fusion = pred[]{:T(512)} fusion(s32[4]{0:T(128)S(1)} %copy-done.3, s32[1]{0:T(128)} %bitcast.7, s32[1]{0:T(128)} %bitcast.6, s32[1]{0:T(128)} %bitcast.5, s32[1]{0:T(128)} %constant.96.clone.1), kind=kLoop, calls=%fused_computation.118 | loop fusion | flops 27 | bytes 33 | tf_op jit(solution)/shard_map/reduce.1
  55.1 18.5 %all-reduce.6.cloned.1.call-done = f32[1,256,256]{2,1,0:T(8,128)} async-done(((f32[1,256,256]{2,1,0:T(8,128)}), f32[1,256,256]{2,1,0:T(8,128)}) %all-reduce.6.cloned.1.call-update) | async-done | bytes 262160 | tf_op jit(solution)/shard_map/psum | solution.py:75
  74.6 1.7 %fusion.21 = f32[256,2,256]{2,0,1:T(8,128)S(1)} fusion(f32[2,256,256]{2,1,0:T(8,128)S(1)} %convolution_subtract_fusion.2, f32[256,256]{1,0:T(8,128)S(1)} %multiply_bitcast_fusion.3), kind=kOutput, calls=%fused_computation.46 | convolution fusion | flops 403767296 | bytes 1310720 | tf_op jit(solution)/shard_map/dot_general | solution.py:25
  76.2 1.6 fusion.17
  77.9 1.7 %fusion.2 = f32[2,256,256]{2,1,0:T(8,128)S(1)} fusion(f32[256,2,256]{2,0,1:T(8,128)S(1)} %fusion.17, f32[2,256,256]{2,1,0:T(8,128)S(1)} %convolution_subtract_fusion.2, f32[256,256]{1,0:T(8,128)S(1)} %multiply_bitcast_fusion.3), kind=kOutput, calls=%fused_computation.6 | convolution fusion | flops 404029440 | bytes 1835008 | tf_op jit(solution)/shard_map/dot_general | solution.py:25
  79.6 1.7 %fusion.3 = f32[2,256,256]{2,1,0:T(8,128)S(1)} fusion(f32[256,2,256]{2,0,1:T(8,128)S(1)} %fusion.21, f32[2,256,256]{2,1,0:T(8,128)S(1)} %get-tuple-element.133, f32[256,256]{1,0:T(8,128)S(1)} %multiply_bitcast_fusion.3), kind=kOutput, calls=%fused_computation.8 | convolution fusion | flops 404029440 | bytes 1835008 | tf_op jit(solution)/shard_map/dot_general | solution.py:25
  81.2 1.6 fusion.37
  82.8 1.6 fusion.34
  84.4 1.6 fusion.1
  85.9 1.9 %fusion.12 = (f32[256,256]{1,0:T(8,128)S(1)}, f32[256,256]{1,0:T(8,128)S(1)}, f32[256,256]{1,0:T(8,128)S(1)}) fusion(f32[2,256,256]{2,1,0:T(8,128)S(1)} %fusion.1, f32[2,2,256,256]{3,2,1,0:T(8,128)S(1)} %copy-done.1, f32[2,256,256]{2,1,0:T(8,128)S(1)} %get-tuple-element.121, f32[2,256,256]{2,1,0:T(8,128)S(1)} %fusion.34, f32[2,256,256]{2,1,0:T(8,128)S(1)} %fusion.3), kind=kOutput, calls=%fused_computation.31 | convolution fusion | flops 405405696 | bytes 3932160 | tf_op jit(solution)/shard_map/dot_general | solution.py:25
  87.9 2.2 %all-gather = f32[512,256]{1,0:T(8,128)S(1)} all-gather(f32[256,256]{1,0:T(8,128)S(1)} %get-tuple-element.116), channel_id=2, replica_groups=mesh['tile'=16,'mode'=2] {'mode'}, dimensions={0}, use_global_device_ids=true | all-gather | bytes 786432 | tf_op jit(solution)/shard_map/all_gather | solution.py:47
  90.9 4.8 %scatter.4 = f32[1,3,384,256]{3,2,1,0:T(8,128)S(1)} dynamic-update-slice(f32[1,3,384,256]{3,2,1,0:T(8,128)S(1)} %broadcast_in_dim.32, f32[1,3,256,256]{3,2,1,0:T(8,128)S(1)} %maximum_select_fusion, s32[]{:T(128)} %constant.95.clone.1, s32[]{:T(128)} %constant.95.clone.1, s32[]{:T(128)} %bitcast.50, s32[]{:T(128)} %constant.95.clone.1) | dynamic-update-slice | bytes 1572868 | tf_op jit(solution)/shard_map/vmap(vmap())/scatter | solution.py:89
  96.8 3.8 %collective-permute-start.4 = (f32[1,3,128,256]{3,2,1,0:T(8,128)}, f32[1,3,128,256]{3,2,1,0:T(8,128)}, u32[]{:S(2)}, u32[]{:S(2)}) collective-permute-start(f32[1,3,128,256]{3,2,1,0:T(8,128)} %get-tuple-element.123), channel_id=1, source_target_pairs={{0,2},{2,4},{4,6},{6,8},{8,10},{10,12},{12,14},{14,16},{16,18},{18... | collective-permute-start | bytes 1179656 | tf_op jit(solution)/shard_map/ppermute | solution.py:14
  100.6 3.8 %collective-permute-start.5 = (f32[1,3,128,256]{3,2,1,0:T(8,128)}, f32[1,3,128,256]{3,2,1,0:T(8,128)}, u32[]{:S(2)}, u32[]{:S(2)}) collective-permute-start(f32[1,3,128,256]{3,2,1,0:T(8,128)} %get-tuple-element.122), channel_id=1, source_target_pairs={{0,4},{2,6},{4,8},{6,10},{8,12},{10,14},{12,16},{14,18},{16,20},{1... | collective-permute-start | bytes 1179656 | tf_op jit(solution)/shard_map/ppermute | solution.py:14
  110.4 4.8 %dynamic_update_slice.12 = f32[3,128,2048]{2,1,0:T(8,128)S(1)} dynamic-update-slice(f32[3,128,2048]{2,1,0:T(8,128)S(1)} %broadcast_in_dim.31, f32[3,128,256]{2,1,0:T(8,128)S(1)} %get-tuple-element.124, s32[]{:T(128)} %constant.95.clone.1, s32[]{:T(128)} %constant.95.clone.1, s32[]{:T(128)S(6)} %select_n.101) | dynamic-update-slice | bytes 786436 | tf_op jit(solution)/shard_map/while/body/eval_jaxpr/dynamic_update_slice | solution.py:105
  116.4 4.8 %dynamic_update_slice.13 = f32[3,128,2048]{2,1,0:T(8,128)S(1)} dynamic-update-slice(f32[3,128,2048]{2,1,0:T(8,128)S(1)} %dynamic_update_slice.12, f32[3,128,256]{2,1,0:T(8,128)S(1)} %bitcast_add_fusion.1, s32[]{:T(128)} %constant.95.clone.1, s32[]{:T(128)} %constant.95.clone.1, s32[]{:T(128)S(6)} %select_n.102) | dynamic-update-slice | bytes 786436 | tf_op jit(solution)/shard_map/while/body/eval_jaxpr/dynamic_update_slice | solution.py:105
  122.4 4.8 %dynamic_update_slice.14 = f32[3,128,2048]{2,1,0:T(8,128)S(1)} dynamic-update-slice(f32[3,128,2048]{2,1,0:T(8,128)S(1)} %dynamic_update_slice.13, f32[3,128,256]{2,1,0:T(8,128)S(1)} %bitcast_add_fusion, s32[]{:T(128)} %constant.95.clone.1, s32[]{:T(128)} %constant.95.clone.1, s32[]{:T(128)S(6)} %select_n.103) | dynamic-update-slice | bytes 786436 | tf_op jit(solution)/shard_map/while/body/eval_jaxpr/dynamic_update_slice | solution.py:105
  127.2 1.5 slice.166
  129.8 22.5 %all-reduce.8.cloned.1.call-done = f32[2,128,2048]{2,1,0:T(8,128)} async-done(((f32[2,128,2048]{2,1,0:T(8,128)}), f32[2,128,2048]{2,1,0:T(8,128)}) %all-reduce.8.cloned.1.call-update) | async-done | bytes 2097168 | tf_op jit(solution)/shard_map/psum | solution.py:112
  152.3 4.5 %divide_add_fusion = f32[2,128,2048]{2,1,0:T(8,128)} fusion(f32[2,128,2048]{2,1,0:T(8,128)} %param.8, f32[2,128,2048]{2,1,0:T(8,128)} %all-reduce.8.cloned.1.call-done, f32[128,2048]{1,0:T(8,128)} %fusion.6), kind=kLoop, calls=%fused_computation | loop fusion | flops 1048576 | bytes 7340032 | tf_op jit(solution)/shard_map/add | solution.py:113
  (40 shorter events, 14.4 us)
Async XLA Ops:
  7.2 29.8 %copy-start.1 = (f32[2,2,256,256]{3,2,1,0:T(8,128)S(1)}, f32[2,2,256,256]{3,2,1,0:T(8,128)}, u32[]{:S(2)}) copy-start(f32[2,2,256,256]{3,2,1,0:T(8,128)} %param.9) | copy-start | bytes 3145732
  7.2 66.4 %all-reduce.6.cloned.1.call-start = ((), (), s32[]{:S(2)}) async-start(), calls=%async_computation | async-start | bytes 524288 | tf_op jit(solution)/shard_map/psum | solution.py:75
  9.3 11.2 %collective-permute-start.2 = (s32[1]{0:T(128)}, s32[1]{0:T(128)}, u32[]{:S(2)}, u32[]{:S(2)}) collective-permute-start(s32[1]{0:T(128)} %bitcast.10), channel_id=1, source_target_pairs={{0,4},{2,6},{4,8},{6,10},{8,12},{10,14},{12,16},{14,18},{16,20},{1... | collective-permute-start | bytes 20 | tf_op jit(solution)/shard_map/ppermute | solution.py:14
  14.7 7.1 %collective-permute-start = (s32[1]{0:T(128)}, s32[1]{0:T(128)}, u32[]{:S(2)}, u32[]{:S(2)}) collective-permute-start(s32[1]{0:T(128)} %bitcast.10), channel_id=1, source_target_pairs={{0,2},{2,4},{4,6},{6,8},{8,10},{10,12},{12,14},{14,16},{16,18},{18... | collective-permute-start | bytes 20 | tf_op jit(solution)/shard_map/ppermute | solution.py:14
  26.0 9.4 %collective-permute-start.3 = (f32[1,2,128,256]{3,2,1,0:T(8,128)S(1)}, f32[1,2,128,256]{3,2,1,0:T(8,128)S(1)}, u32[]{:S(2)}, u32[]{:S(2)}) collective-permute-start(f32[1,2,128,256]{3,2,1,0:T(8,128)S(1)} %get-tuple-element.117), channel_id=1, source_target_pairs={{4,0},{6,2},{8,4},{10,6},{12,8},{14,10},{16,12},{18,14},{20,16},{2... | collective-permute-start | bytes 786440 | tf_op jit(solution)/shard_map/ppermute | solution.py:14
  27.3 9.4 %collective-permute-start.1 = (f32[1,2,128,256]{3,2,1,0:T(8,128)S(1)}, f32[1,2,128,256]{3,2,1,0:T(8,128)S(1)}, u32[]{:S(2)}, u32[]{:S(2)}) collective-permute-start(f32[1,2,128,256]{3,2,1,0:T(8,128)S(1)} %get-tuple-element.118), channel_id=1, source_target_pairs={{2,0},{4,2},{6,4},{8,6},{10,8},{12,10},{14,12},{16,14},{18,16},{20... | collective-permute-start | bytes 786440 | tf_op jit(solution)/shard_map/ppermute | solution.py:14
  46.8 4.2 %copy-start.4 = (s32[1,3]{1,0:T(1,128)S(1)}, s32[1,3]{1,0:T(1,128)}, u32[]{:S(2)}) copy-start(s32[1,3]{1,0:T(1,128)} %constant.105.clone.1) | copy-start | bytes 40
  46.8 5.6 %copy-start.3 = (s32[4]{0:T(128)S(1)}, s32[4]{0:T(128)}, u32[]{:S(2)}) copy-start(s32[4]{0:T(128)} %constant.106.clone.1) | copy-start | bytes 52
  46.9 26.7 %copy-start.2 = (f32[1,256,256]{2,1,0:T(8,128)S(1)}, f32[1,256,256]{2,1,0:T(8,128)}, u32[]{:S(2)}) copy-start(f32[1,256,256]{2,1,0:T(8,128)} %param.10) | copy-start | bytes 786436
  50.9 101.3 %all-reduce.8.cloned.1.call-start = ((), (), s32[]{:S(2)}) async-start(), calls=%async_computation.1 | async-start | bytes 4194304 | tf_op jit(solution)/shard_map/psum | solution.py:112
  96.8 18.4 %collective-permute-start.4 = (f32[1,3,128,256]{3,2,1,0:T(8,128)}, f32[1,3,128,256]{3,2,1,0:T(8,128)}, u32[]{:S(2)}, u32[]{:S(2)}) collective-permute-start(f32[1,3,128,256]{3,2,1,0:T(8,128)} %get-tuple-element.123), channel_id=1, source_target_pairs={{0,2},{2,4},{4,6},{6,8},{8,10},{10,12},{12,14},{14,16},{16,18},{18... | collective-permute-start | bytes 1179656 | tf_op jit(solution)/shard_map/ppermute | solution.py:14
  100.6 20.6 %collective-permute-start.5 = (f32[1,3,128,256]{3,2,1,0:T(8,128)}, f32[1,3,128,256]{3,2,1,0:T(8,128)}, u32[]{:S(2)}, u32[]{:S(2)}) collective-permute-start(f32[1,3,128,256]{3,2,1,0:T(8,128)} %get-tuple-element.122), channel_id=1, source_target_pairs={{0,4},{2,6},{4,8},{6,10},{8,12},{10,14},{12,16},{14,18},{16,20},{1... | collective-permute-start | bytes 1179656 | tf_op jit(solution)/shard_map/ppermute | solution.py:14
  152.3 4.5 %copy-start = (f32[2,128,2048]{2,1,0:T(8,128)S(1)}, f32[2,128,2048]{2,1,0:T(8,128)}, u32[]{:S(2)}) copy-start(f32[2,128,2048]{2,1,0:T(8,128)} %all-reduce.8.cloned.1.call-done) | copy-start | bytes 6291460
Sparse Core Ops, SparseCore 0:
  51.1 22.4 all-reduce.5
  128.9 23.3 all-reduce.7
